TPU v7x, 32 devices: a whole 2x2x4 slice. The times are simulated.
32 devices in a mesh: dp: 8 (over z, x), tensor: 4 (over y, core).
Axes of the slice: x: 2, y: 2, z: 4, core: 2. Of those that a mesh axis runs over, the one named last changes fastest.
Arguments:
- embedded: bfloat16 [8192, 768], P(('dp', 'tensor')), may hold values from -6 to 6
- bigram_ids: int32 [8192], P(('dp', 'tensor')), may hold values from 0 to 16383, as said below
- trigram_ids: int32 [8192], P(('dp', 'tensor')), may hold values from 0 to 16383, as said below
- prefix_lens: int32 [8], P('dp'), may hold values from 102 to 512
- bigram_table: bfloat16 [16384, 192], P('dp'), may hold values from -6 to 6
- trigram_table: bfloat16 [16384, 192], P('dp'), may hold values from -6 to 6
- ngram_weight: bfloat16 [384, 768], replicated, may hold values from -0.3125 to 0.3125
- first_gain: float32 [768], replicated, may hold values from 0.5 to 1.5
- attend_weight: bfloat16 [768, 2304], P(None, 'tensor'), may hold values from -0.21875 to 0.21875
- output_weight: bfloat16 [768, 768], P('tensor'), may hold values from -0.875 to 0.875
- second_gain: float32 [768], replicated, may hold values from 0.5 to 1.5
- gate_weight: bfloat16 [768, 2048], P(None, 'tensor'), may hold values from -0.21875 to 0.21875
- up_weight: bfloat16 [768, 2048], P(None, 'tensor'), may hold values from -0.21875 to 0.21875
- down_weight: bfloat16 [2048, 768], P('tensor'), may hold values from -0.125 to 0.125
- cotangent: bfloat16 [8192, 768], P('dp'), may hold values from -6 to 6
Outputs:
- block_out: bfloat16 [8192, 768], P(('dp', 'tensor'))
- embed_grad: float32 [8192, 768], P(('dp', 'tensor'))
- bigram_grad: float32 [16384, 192], P(('dp', 'tensor'))
- trigram_grad: float32 [16384, 192], P(('dp', 'tensor'))
- ngram_weight_grad: float32 [384, 768], P(None, ('dp', 'tensor'))
- first_gain_grad: float32 [768], P(('dp', 'tensor'))
- attend_weight_grad: float32 [768, 2304], P('dp', 'tensor')
- output_weight_grad: float32 [768, 768], P('tensor', 'dp')
- second_gain_grad: float32 [768], P(('dp', 'tensor'))
- gate_weight_grad: float32 [768, 2048], P('dp', 'tensor')
- up_weight_grad: float32 [768, 2048], P('dp', 'tensor')
- down_weight_grad: float32 [2048, 768], P('tensor', 'dp')
Inputs may be any that keep to these rules, and one draw needn't show every extreme that they name: `bigram_ids`: row r of the 2-gram table is held by index r // 2048 of dp. Among the tokens of one device, at most 64 name rows of one holder; in every draw one holder gets exactly 64 from every device. `trigram_ids`: row r of the 3-gram table is held by index r // 2048 of dp. Among the tokens of one device, at most 64 name rows of one holder; in every draw one holder gets exactly 64 from every device.
All inputs are finite; a program needn't handle non-finite values.
Results may differ from a plain program's by a relative error of at most 0.022.
Values may be sent and summed in bfloat16 or wider, within the bound.
A program may use at most 128 MiB of HBM per device.

v0:
```python
import math
import jax
import jax.numpy as jnp
from jax import lax
from jax.sharding import PartitionSpec as P

HD = 64


def normed_rows(values_in, gain):
    scaling = lax.rsqrt(jnp.mean(values_in * values_in, axis=-1, keepdims=True) + 1e-05)
    return (values_in * scaling * gain, scaling)


def norm_backward(grad_out, values_in, scaling, gain):
    scaled = grad_out * gain
    gain_grad = jnp.sum(grad_out * values_in * scaling, axis=0)
    row_grad = scaling * scaled - values_in * scaling**3 * jnp.mean(
        scaled * values_in, axis=-1, keepdims=True
    )
    return (row_grad, gain_grad)


def rotary_tables(length, width):
    halfway = width // 2
    frequency = jnp.exp(jnp.arange(halfway, dtype=jnp.float32) * (-2.0 * math.log(10000.0) / width))
    angles = jnp.arange(length, dtype=jnp.float32)[:, None] * frequency[None, :]
    return (jnp.cos(angles), jnp.sin(angles))


def rotate(values_in, cosine, sines):
    halfway = values_in.shape[-1] // 2
    leading = values_in[..., :halfway]
    trailing = values_in[..., halfway:]
    cosine = cosine[:, None, :]
    sines = sines[:, None, :]
    return jnp.concatenate(
        [leading * cosine - trailing * sines, trailing * cosine + leading * sines], axis=-1
    )


def unrotate(grads, cosine, sines):
    halfway = grads.shape[-1] // 2
    leading = grads[..., :halfway]
    trailing = grads[..., halfway:]
    cosine = cosine[:, None, :]
    sines = sines[:, None, :]
    return jnp.concatenate(
        [leading * cosine + trailing * sines, trailing * cosine - leading * sines], axis=-1
    )


def inner(left, right):
    return lax.dot_general(
        left, right, (((0,), (0,)), ((), ())), preferred_element_type=jnp.float32
    )


def slot_positions(row_ids, rows_dev, peer_count, capacity):
    owner = row_ids // rows_dev
    onehot = (owner[:, None] == jnp.arange(peer_count)[None, :]).astype(jnp.float32)
    tokens = row_ids.shape[0]
    earlier = (jnp.arange(tokens)[None, :] < jnp.arange(tokens)[:, None]).astype(jnp.float32)
    ranks = jnp.dot(earlier, onehot, precision=lax.Precision.HIGHEST)
    slot = jnp.sum(ranks * onehot, axis=1).astype(jnp.int32)
    return owner * capacity + slot


def shards(
    embedded,
    bigram_ids,
    trigram_ids,
    prefix_lens,
    bigram_table,
    trigram_table,
    ngram_weight,
    first_gain,
    attend_weight,
    output_weight,
    second_gain,
    gate_weight,
    up_weight,
    down_weight,
    cotangent,
):
    peer_count = lax.axis_size("dp")
    split_count = lax.axis_size("tensor")
    local_rows = embedded.shape[0]
    length = local_rows * split_count
    rows_dev = bigram_table.shape[0]
    table_width = bigram_table.shape[1]
    capacity = max(4, 2 * local_rows // peer_count)
    scaling_factor = HD ** (-0.5)
    bigram_slot = slot_positions(bigram_ids, rows_dev, peer_count, capacity)
    trigram_slot = slot_positions(trigram_ids, rows_dev, peer_count, capacity)
    requests = jnp.zeros((2, peer_count * capacity), jnp.int32)
    requests = requests.at[0, bigram_slot].set(bigram_ids % rows_dev + 1)
    requests = requests.at[1, trigram_slot].set(trigram_ids % rows_dev + 1)
    requests = requests.reshape(2, peer_count, capacity)
    asked_rows = lax.all_to_all(requests, "dp", split_axis=1, concat_axis=1, tiled=True)
    picked = jnp.maximum(asked_rows - 1, 0)
    found_rows = jnp.stack([bigram_table[picked[0]], trigram_table[picked[1]]])
    answer = lax.all_to_all(found_rows, "dp", split_axis=1, concat_axis=1, tiled=True)
    fetched, asked_rows = (answer, asked_rows)
    fetched = fetched.reshape(2, peer_count * capacity, table_width)
    ngram_rows = jnp.concatenate([fetched[0][bigram_slot], fetched[1][trigram_slot]], axis=1)
    lifted = jnp.dot(ngram_rows, ngram_weight, preferred_element_type=jnp.float32)
    inputs = embedded.astype(jnp.float32) + lifted
    normed_one, first_scale = normed_rows(inputs, first_gain)
    normed_one_full = lax.all_gather(normed_one.astype(jnp.bfloat16), "tensor", axis=0, tiled=True)
    head_count = attend_weight.shape[1] // (3 * HD)
    mixture = jnp.dot(normed_one_full, attend_weight, preferred_element_type=jnp.float32)
    mixture = mixture.reshape(length, head_count, 3, HD)
    cosine, sines = rotary_tables(length, HD)
    queries = rotate(mixture[:, :, 0], cosine, sines).astype(jnp.bfloat16)
    keys = rotate(mixture[:, :, 1], cosine, sines).astype(jnp.bfloat16)
    values = mixture[:, :, 2].astype(jnp.bfloat16)
    block_size = min(512, length)
    block_count = length // block_size
    prefix = prefix_lens[0]
    key_position = jnp.arange(length)

    def scores_of(query_block, offset):
        products = (
            jnp.einsum("qhd,khd->hqk", query_block, keys, preferred_element_type=jnp.float32)
            * scaling_factor
        )
        query_position = offset + jnp.arange(block_size)
        allowed = (key_position[None, :] <= query_position[:, None]) | (
            key_position[None, :] < prefix
        )
        return jnp.where(allowed[None], products, -1000000000.0)

    def forward_block(position):
        offset = position * block_size
        query_block = lax.dynamic_slice_in_dim(queries, offset, block_size, 0)
        scores = scores_of(query_block, offset)
        highest_score = jnp.max(scores, axis=-1, keepdims=True)
        powers = jnp.exp(scores - highest_score)
        totals = jnp.sum(powers, axis=-1, keepdims=True)
        weights_low = (powers / totals).astype(jnp.bfloat16)
        result = jnp.einsum("hqk,khd->qhd", weights_low, values, preferred_element_type=jnp.float32)
        return (result.astype(jnp.bfloat16), (highest_score + jnp.log(totals))[..., 0])

    attended, log_totals = lax.map(forward_block, jnp.arange(block_count))
    attended = attended.reshape(length, head_count * HD)
    part_rows = attended
    branch_one = lax.psum_scatter(
        jnp.dot(part_rows, output_weight, preferred_element_type=jnp.float32).astype(jnp.bfloat16),
        "tensor",
        scatter_dimension=0,
        tiled=True,
    ).astype(jnp.float32)
    after = inputs + branch_one
    normed_two, second_scale = normed_rows(after, second_gain)
    normed_two_full = lax.all_gather(normed_two.astype(jnp.bfloat16), "tensor", axis=0, tiled=True)
    gate = jnp.dot(normed_two_full, gate_weight, preferred_element_type=jnp.float32)
    up_part = jnp.dot(normed_two_full, up_weight, preferred_element_type=jnp.float32)
    sigmoid_gate = jax.nn.sigmoid(gate)
    activity = (gate * sigmoid_gate * up_part).astype(jnp.bfloat16)
    part_rows = activity
    branch_two = lax.psum_scatter(
        jnp.dot(part_rows, down_weight, preferred_element_type=jnp.float32).astype(jnp.bfloat16),
        "tensor",
        scatter_dimension=0,
        tiled=True,
    ).astype(jnp.float32)
    block_out = (after + branch_two).astype(jnp.bfloat16)
    own_cot = lax.dynamic_slice_in_dim(
        cotangent, lax.axis_index("tensor") * local_rows, local_rows, 0
    ).astype(jnp.float32)
    down_grad = inner(activity, cotangent)
    activity_back = jnp.dot(cotangent, down_weight.T, preferred_element_type=jnp.float32)
    gate_back = (
        activity_back * up_part * sigmoid_gate * (1.0 + gate * (1.0 - sigmoid_gate))
    ).astype(jnp.bfloat16)
    up_back = (activity_back * gate * sigmoid_gate).astype(jnp.bfloat16)
    gate_grad = inner(normed_two_full, gate_back)
    up_grad = inner(normed_two_full, up_back)
    normed_two_back = lax.psum_scatter(
        (
            jnp.dot(gate_back, gate_weight.T, preferred_element_type=jnp.float32)
            + jnp.dot(up_back, up_weight.T, preferred_element_type=jnp.float32)
        ).astype(jnp.bfloat16),
        "tensor",
        scatter_dimension=0,
        tiled=True,
    ).astype(jnp.float32)
    second_row_grad, second_partial = norm_backward(
        normed_two_back, after, second_scale, second_gain
    )
    after_grad = own_cot + second_row_grad
    attn_back_full = lax.all_gather(after_grad.astype(jnp.bfloat16), "tensor", axis=0, tiled=True)
    output_grad = inner(attended, attn_back_full)
    attended_back = jnp.dot(
        attn_back_full, output_weight.T, preferred_element_type=jnp.float32
    ).astype(jnp.bfloat16)
    attended_back = attended_back.reshape(length, head_count, HD)

    def backward_block(carry, item):
        key_sum, value_sum = carry
        position, log_block = item
        offset = position * block_size
        query_block = lax.dynamic_slice_in_dim(queries, offset, block_size, 0)
        grad_block = lax.dynamic_slice_in_dim(attended_back, offset, block_size, 0)
        probs = jnp.exp(scores_of(query_block, offset) - log_block[..., None])
        prob_back = jnp.einsum(
            "qhd,khd->hqk", grad_block, values, preferred_element_type=jnp.float32
        )
        centre = jnp.sum(probs * prob_back, axis=-1, keepdims=True)
        score_back = (probs * (prob_back - centre)).astype(jnp.bfloat16)
        query_grad = (
            jnp.einsum("hqk,khd->qhd", score_back, keys, preferred_element_type=jnp.float32)
            * scaling_factor
        )
        key_sum = (
            key_sum
            + jnp.einsum(
                "hqk,qhd->khd", score_back, query_block, preferred_element_type=jnp.float32
            )
            * scaling_factor
        )
        value_sum = value_sum + jnp.einsum(
            "hqk,qhd->khd",
            probs.astype(jnp.bfloat16),
            grad_block,
            preferred_element_type=jnp.float32,
        )
        return ((key_sum, value_sum), query_grad)

    zero_heads = jnp.zeros((length, head_count, HD), jnp.float32)
    (key_sum, value_sum), query_grads = lax.scan(
        backward_block, (zero_heads, zero_heads), (jnp.arange(block_count), log_totals)
    )
    query_back = (
        query_grads.reshape(length, head_count, HD).astype(jnp.bfloat16).astype(jnp.float32)
    )
    key_back = key_sum.astype(jnp.bfloat16).astype(jnp.float32)
    mixture_back = jnp.stack(
        [unrotate(query_back, cosine, sines), unrotate(key_back, cosine, sines), value_sum], axis=2
    )
    mixture_back = mixture_back.reshape(length, head_count * 3 * HD).astype(jnp.bfloat16)
    attend_grad = inner(normed_one_full, mixture_back)
    part_rows = mixture_back
    normed_one_back = lax.psum_scatter(
        jnp.dot(part_rows, attend_weight.T, preferred_element_type=jnp.float32).astype(
            jnp.bfloat16
        ),
        "tensor",
        scatter_dimension=0,
        tiled=True,
    ).astype(jnp.float32)
    first_row_grad, first_partial = norm_backward(normed_one_back, inputs, first_scale, first_gain)
    embed_grad = after_grad + first_row_grad
    lifted_back = embed_grad.astype(jnp.bfloat16)
    ngram_partial = inner(ngram_rows, lifted_back)
    row_back = jnp.dot(lifted_back, ngram_weight.T, preferred_element_type=jnp.float32)
    outgoing = jnp.zeros((2, peer_count * capacity, table_width), jnp.float32)
    outgoing = outgoing.at[0, bigram_slot].set(row_back[:, :table_width])
    outgoing = outgoing.at[1, trigram_slot].set(row_back[:, table_width:])
    outgoing = outgoing.reshape(2, peer_count, capacity, table_width)
    arrived = lax.all_to_all(
        outgoing.astype(jnp.bfloat16), "dp", split_axis=1, concat_axis=1, tiled=True
    ).astype(outgoing.dtype)
    picked_rows = jnp.maximum(asked_rows - 1, 0)
    bigram_part = (
        jnp.zeros((rows_dev, table_width), jnp.float32)
        .at[picked_rows[0].reshape(-1)]
        .add(arrived[0].reshape(-1, table_width))
    )
    trigram_part = (
        jnp.zeros((rows_dev, table_width), jnp.float32)
        .at[picked_rows[1].reshape(-1)]
        .add(arrived[1].reshape(-1, table_width))
    )
    attend_sum, output_sum, gate_sum, up_sum, down_sum, ngram_group, first_group, second_group = (
        lax.psum_scatter(attend_grad, "dp", scatter_dimension=0, tiled=True),
        lax.psum_scatter(output_grad, "dp", scatter_dimension=1, tiled=True),
        lax.psum_scatter(gate_grad, "dp", scatter_dimension=0, tiled=True),
        lax.psum_scatter(up_grad, "dp", scatter_dimension=0, tiled=True),
        lax.psum_scatter(down_grad, "dp", scatter_dimension=1, tiled=True),
        lax.psum_scatter(ngram_partial, "dp", scatter_dimension=1, tiled=True),
        lax.psum_scatter(first_partial, "dp", scatter_dimension=0, tiled=True),
        lax.psum_scatter(second_partial, "dp", scatter_dimension=0, tiled=True),
    )
    bigram_grad, trigram_grad, ngram_grad, first_grad, second_grad = (
        lax.psum_scatter(
            bigram_part.astype(jnp.bfloat16), "tensor", scatter_dimension=0, tiled=True
        ).astype(jnp.float32),
        lax.psum_scatter(
            trigram_part.astype(jnp.bfloat16), "tensor", scatter_dimension=0, tiled=True
        ).astype(jnp.float32),
        lax.psum_scatter(
            ngram_group.astype(jnp.bfloat16), "tensor", scatter_dimension=1, tiled=True
        ).astype(jnp.float32),
        lax.psum_scatter(
            first_group.astype(jnp.bfloat16), "tensor", scatter_dimension=0, tiled=True
        ).astype(jnp.float32),
        lax.psum_scatter(
            second_group.astype(jnp.bfloat16), "tensor", scatter_dimension=0, tiled=True
        ).astype(jnp.float32),
    )
    return (
        block_out,
        embed_grad,
        bigram_grad,
        trigram_grad,
        ngram_grad,
        first_grad,
        attend_sum,
        output_sum,
        second_grad,
        gate_sum,
        up_sum,
        down_sum,
    )


def solution(mesh):
    placed = (
        P(("dp", "tensor"), None),
        P(("dp", "tensor")),
        P(("dp", "tensor")),
        P("dp"),
        P("dp", None),
        P("dp", None),
        P(),
        P(),
        P(None, "tensor"),
        P("tensor", None),
        P(),
        P(None, "tensor"),
        P(None, "tensor"),
        P("tensor", None),
        P("dp", None),
    )
    return jax.shard_map(
        shards,
        mesh=mesh,
        in_specs=placed,
        out_specs=(
            P(("dp", "tensor"), None),
            P(("dp", "tensor"), None),
            P(("dp", "tensor"), None),
            P(("dp", "tensor"), None),
            P(None, ("dp", "tensor")),
            P(("dp", "tensor")),
            P("dp", "tensor"),
            P("tensor", "dp"),
            P(("dp", "tensor")),
            P("dp", "tensor"),
            P("dp", "tensor"),
            P("tensor", "dp"),
        ),
        check_vma=False,
    )
```

profile of v0, /device:TPU:0, one launch (start us, length us, event | category | flops | bytes accessed | tf_op | source)
XLA Modules:
  0.0 817.6 jit_solution(4274439268550508631)
XLA Ops:
  9.2 12.4 %scatter_fusion = s32[2,512]{1,0:T(2,128)S(1)} fusion(s32[2,512]{1,0:T(2,128)S(1)} %broadcast_in_dim.44, s32[256]{0:T(256)S(1)} %bitcast.157, s32[256]{0:T(256)S(1)} %get-tuple-element.362), kind=kCustom, calls=%fused_computation.4 | custom fusion | bytes 5120 | tf_op jit(solution)/shard_map/scatter | solution.py:97
  21.6 12.4 %scatter_fusion.1 = s32[2,512]{1,0:T(2,128)S(1)} fusion(s32[2,512]{1,0:T(2,128)S(1)} %scatter_fusion, s32[256]{0:T(256)S(1)} %bitcast.159, s32[256]{0:T(256)S(1)} %get-tuple-element.360), kind=kCustom, calls=%fused_computation.5 | custom fusion | bytes 5120 | tf_op jit(solution)/shard_map/scatter | solution.py:98
  34.7 7.3 all-to-all-start
  44.0 4.4 all-to-all-done
  58.9 13.2 %all-to-all-done.1 = bf16[2,8,64,192]{3,2,0,1:T(8,128)(2,1)S(1)} async-done(((bf16[2,8,64,192]{3,2,0,1:T(8,128)(2,1)}), bf16[2,8,64,192]{3,2,0,1:T(8,128)(2,1)S(1)}, u32[]{:S(2)}, u32[]{:S(2)}) %all-to-all-start.1) | async-done | bytes 393248 | tf_op jit(solution)/shard_map/all_to_all | solution.py:103
  77.7 17.7 %all-gather.4.cloned.1.call-done = bf16[1024,768]{1,0:T(8,128)(2,1)} async-done(((bf16[256,768]{1,0:T(8,128)(2,1)}), bf16[1024,768]{1,0:T(8,128)(2,1)}) %all-gather.4.cloned.1.call-update) | async-done | bytes 1572880 | tf_op jit(solution)/shard_map/all_gather | solution.py:110
  98.7 15.5 %while.30 = (s32[]{:T(128)}, bf16[2,512,3,64]{1,3,2,0:T(8,128)(2,1)S(1)}, f32[2,3,512]{2,1,0:T(4,128)S(1)}, s32[2]{0:T(128)S(1)}, s32[]{:T(128)}, /*index=5*/bf1...) while((s32[]{:T(128)}, ...), condition=%wide.region_8.9_spmd.clone.clone, body=%wide.region_5.8_spmd.clone.clone.sunk | while | flops 422674432 | bytes 22216908 | solution.py:145
  118.4 28.3 %reduce-scatter.18.cloned.1.call-done = bf16[256,768]{1,0:T(8,128)(2,1)} async-done(((bf16[1024,768]{1,0:T(8,128)(2,1)}), bf16[256,768]{1,0:T(8,128)(2,1)}) %reduce-scatter.18.cloned.1.call-update) | async-done | bytes 393232 | tf_op jit(solution)/shard_map/reduce_scatter | solution.py:148
  150.4 19.8 %all-gather.6.cloned.1.call-done = bf16[1024,768]{1,0:T(8,128)(2,1)} async-done(((bf16[256,768]{1,0:T(8,128)(2,1)}), bf16[1024,768]{1,0:T(8,128)(2,1)}) %all-gather.6.cloned.1.call-update) | async-done | bytes 1572880 | tf_op jit(solution)/shard_map/all_gather | solution.py:156
  181.3 28.3 %reduce-scatter.22.cloned.1.call-done = bf16[256,768]{1,0:T(8,128)(2,1)} async-done(((bf16[1024,768]{1,0:T(8,128)(2,1)}), bf16[256,768]{1,0:T(8,128)(2,1)}) %reduce-scatter.22.cloned.1.call-update) | async-done | bytes 393232 | tf_op jit(solution)/shard_map/reduce_scatter | solution.py:180
  213.9 19.6 %all-gather.8.cloned.1.call-done = bf16[1024,768]{1,0:T(8,128)(2,1)} async-done(((bf16[256,768]{1,0:T(8,128)(2,1)}), bf16[1024,768]{1,0:T(8,128)(2,1)}) %all-gather.8.cloned.1.call-update) | async-done | bytes 1572880 | tf_op jit(solution)/shard_map/all_gather | solution.py:193
  236.3 23.7 %while.31 = (s32[]{:T(128)}, f32[1024,3,64]{0,2,1:T(8,128)S(1)}, f32[1024,3,64]{0,2,1:T(8,128)}, bf16[2,512,3,64]{1,3,2,0:T(8,128)(2,1)}, s32[2]{0:T(128)S(1)}, ...) while((s32[]{:T(128)}, f32[1024,3,64]{0,2,1:T(8,128)S(1)}, ...), condition=%wide.region_16.17_spmd.clone.clone, body=%wide.region_14.16_spmd.clone.clone.sunk | while | flops 1032355840 | bytes 67424672 | solution.py:232
  269.0 25.8 %reduce-scatter.24.cloned.1.call-done = bf16[256,768]{1,0:T(8,128)(2,1)} async-done(((bf16[1024,768]{1,0:T(8,128)(2,1)}), bf16[256,768]{1,0:T(8,128)(2,1)}) %reduce-scatter.24.cloned.1.call-update) | async-done | bytes 393232 | tf_op jit(solution)/shard_map/reduce_scatter | solution.py:245
  296.0 29.6 %reduce-scatter.20.cloned.1.call-done = bf16[256,768]{1,0:T(8,128)(2,1)} async-done(((bf16[1024,768]{1,0:T(8,128)(2,1)}), bf16[256,768]{1,0:T(8,128)(2,1)}) %reduce-scatter.20.cloned.1.call-update) | async-done | bytes 393232 | tf_op jit(solution)/shard_map/reduce_scatter | solution.py:162
  333.6 13.1 %scatter_fusion.2 = f32[2,512,192]{2,1,0:T(8,128)S(1)} fusion(f32[2,512,192]{2,1,0:T(8,128)S(1)} %broadcast_in_dim.58, s32[256]{0:T(256)S(1)} %bitcast.158, f32[256,192]{1,0:T(8,128)S(1)} %get-tuple-element.347), kind=kCustom, calls=%fused_computation.6 | custom fusion | bytes 591872 | tf_op jit(solution)/shard_map/scatter | solution.py:259
  346.7 13.1 %scatter_fusion.3 = f32[2,512,192]{2,1,0:T(8,128)S(1)} fusion(f32[2,512,192]{2,1,0:T(8,128)S(1)} %scatter_fusion.2, s32[256]{0:T(256)S(1)} %bitcast.160, f32[256,192]{1,0:T(8,128)S(1)} %get-tuple-element.346), kind=kCustom, calls=%fused_computation.7 | custom fusion | bytes 591872 | tf_op jit(solution)/shard_map/scatter | solution.py:260
  360.8 5.5 all-to-all-start.2
  366.4 14.4 %all-to-all-done.2 = bf16[2,8,64,192]{3,2,0,1:T(8,128)(2,1)S(1)} async-done(((bf16[2,8,64,192]{3,2,0,1:T(8,128)(2,1)}), bf16[2,8,64,192]{3,2,0,1:T(8,128)(2,1)S(1)}, u32[]{:S(2)}, u32[]{:S(2)}) %all-to-all-start.2) | async-done | bytes 393248 | tf_op jit(solution)/shard_map/all_to_all | solution.py:262
  381.7 4.6 scatter_custom_fusion.4
  387.5 4.1 scatter_custom_fusion.5
  397.5 4.1 fusion.89
  404.2 4.1 fusion.91
  408.4 4.1 fusion.88
  415.0 45.6 %reduce-scatter.40.cloned.1.call-done = f32[96,192]{1,0:T(8,128)} async-done(((f32[768,192]{1,0:T(8,128)}), f32[96,192]{1,0:T(8,128)}) %reduce-scatter.40.cloned.1.call-update) | async-done | bytes 73744
  462.2 19.6 %all-reduce.7 = (bf16[768]{0:T(1024)(128)(2,1)S(1)}, bf16[768]{0:T(1024)(128)(2,1)S(1)}) all-reduce(f32[768]{0:T(1024)S(1)} %get-tuple-element.279, f32[768]{0:T(1024)S(1)} %copy-done.50), channel_id=10, replica_groups=mesh['dp'=8,'tensor'=4] {'dp'}, use_global_device_ids=true, to_apply=%region_28.29.clone | all-reduce | flops 1536 | bytes 9216
  482.0 5.6 all-reduce.8
  490.6 24.0 %reduce-scatter.28.cloned.1.call-done = bf16[512,192]{1,0:T(8,128)(2,1)} async-done(((bf16[2048,192]{1,0:T(8,128)(2,1)}), bf16[512,192]{1,0:T(8,128)(2,1)}) %reduce-scatter.28.cloned.1.call-update) | async-done | bytes 196624 | tf_op jit(solution)/shard_map/reduce_scatter | solution.py:290
  516.5 19.7 %reduce-scatter.42.cloned.1.call-done = bf16[384,24]{0,1:T(8,128)(2,1)} async-done(((bf16[384,96]{0,1:T(8,128)(2,1)}), bf16[384,24]{0,1:T(8,128)(2,1)}) %reduce-scatter.42.cloned.1.call-update) | async-done | bytes 18448
  537.5 67.9 %reduce-scatter.34.cloned.1.call-done = f32[96,512]{1,0:T(8,128)} async-done(((f32[768,512]{1,0:T(8,128)}), f32[96,512]{1,0:T(8,128)}) %reduce-scatter.34.cloned.1.call-update) | async-done | bytes 196624 | tf_op jit(solution)/shard_map/reduce_scatter | solution.py:279
  605.4 67.6 %reduce-scatter.36.cloned.1.call-done = f32[96,512]{1,0:T(8,128)} async-done(((f32[768,512]{1,0:T(8,128)}), f32[96,512]{1,0:T(8,128)}) %reduce-scatter.36.cloned.1.call-update) | async-done | bytes 196624 | tf_op jit(solution)/shard_map/reduce_scatter | solution.py:280
  673.0 68.0 %reduce-scatter.38.cloned.1.call-done = f32[512,96]{0,1:T(8,128)} async-done(((f32[512,768]{0,1:T(8,128)}), f32[512,96]{0,1:T(8,128)}) %reduce-scatter.38.cloned.1.call-update) | async-done | bytes 196624 | tf_op jit(solution)/shard_map/reduce_scatter | solution.py:281
  741.0 69.7 %reduce-scatter.32.cloned.1.call-done = f32[96,576]{1,0:T(8,128)} async-done(((f32[768,576]{1,0:T(8,128)}), f32[96,576]{1,0:T(8,128)}) %reduce-scatter.32.cloned.1.call-update) | async-done | bytes 221200 | tf_op jit(solution)/shard_map/reduce_scatter | solution.py:277
  (321 shorter events, 124.5 us)
Async XLA Ops:
  7.2 88.3 %copy-start = (bf16[768,576]{0,1:T(8,128)(2,1)S(1)}, bf16[768,576]{0,1:T(8,128)(2,1)}, u32[]{:S(2)}) copy-start(bf16[768,576]{0,1:T(8,128)(2,1)} %param.27) | copy-start | bytes 2654212
  9.1 32.9 %copy-start.29 = (bf16[2048,192]{0,1:T(8,128)(2,1)S(1)}, bf16[2048,192]{0,1:T(8,128)(2,1)}, u32[]{:S(2)}) copy-start(bf16[2048,192]{0,1:T(8,128)(2,1)} %param.23) | copy-start | bytes 2359300
  34.7 13.7 %all-to-all-start = ((s32[8,1,128]{2,1,0:T(1,128)}), s32[8,1,128]{2,1,0:T(1,128)S(1)}, u32[]{:S(2)}, u32[]{:S(2)}) async-start(s32[8,1,128]{2,1,0:T(1,128)} %reshape.467), calls=%async_computation | async-start | bytes 8192 | tf_op jit(solution)/shard_map/all_to_all | solution.py:100
  55.2 16.9 %all-to-all-start.1 = ((bf16[2,8,64,192]{3,2,0,1:T(8,128)(2,1)}), bf16[2,8,64,192]{3,2,0,1:T(8,128)(2,1)S(1)}, u32[]{:S(2)}, u32[]{:S(2)}) async-start(bf16[2,8,64,192]{3,2,0,1:T(8,128)(2,1)} %pad_maximum_fusion.1), calls=%async_computation.1 | async-start | bytes 1048576 | tf_op jit(solution)/shard_map/all_to_all | solution.py:103
  58.9 36.6 %all-gather.4.cloned.1.call-start = ((), (), s32[]{:S(2)}) async-start(), calls=%async_computation.16 | async-start | bytes 1966080 | tf_op jit(solution)/shard_map/all_gather | solution.py:110
  76.5 70.1 %reduce-scatter.18.cloned.1.call-start = ((), (), s32[]{:S(2)}) async-start(), calls=%async_computation.17 | async-start | bytes 1966080 | tf_op jit(solution)/shard_map/reduce_scatter | solution.py:148
  115.5 32.9 %copy-start.42 = (f32[768]{0:T(1024)S(1)}, f32[768]{0:T(1024)}, u32[]{:S(2)}) copy-start(f32[768]{0:T(1024)} %param.29) | copy-start | bytes 9220
  118.3 51.8 %all-gather.6.cloned.1.call-start = ((), (), s32[]{:S(2)}) async-start(), calls=%async_computation.18 | async-start | bytes 1966080 | tf_op jit(solution)/shard_map/all_gather | solution.py:156
  150.3 59.2 %reduce-scatter.22.cloned.1.call-start = ((), (), s32[]{:S(2)}) async-start(), calls=%async_computation.20 | async-start | bytes 1966080 | tf_op jit(solution)/shard_map/reduce_scatter | solution.py:180
  181.2 52.3 %all-gather.8.cloned.1.call-start = ((), (), s32[]{:S(2)}) async-start(), calls=%async_computation.21 | async-start | bytes 1966080 | tf_op jit(solution)/shard_map/all_gather | solution.py:193
  181.3 52.2 %copy-start.39 = (bf16[192,768]{1,0:T(8,128)(2,1)S(1)}, bf16[192,768]{1,0:T(8,128)(2,1)}, u32[]{:S(2)}) copy-start(bf16[192,768]{1,0:T(8,128)(2,1)} %param.28) | copy-start | bytes 884740
  213.6 81.1 %reduce-scatter.24.cloned.1.call-start = ((), (), s32[]{:S(2)}) async-start(), calls=%async_computation.22 | async-start | bytes 1966080 | tf_op jit(solution)/shard_map/reduce_scatter | solution.py:245
  266.4 59.2 %reduce-scatter.20.cloned.1.call-start = ((), (), s32[]{:S(2)}) async-start(), calls=%async_computation.19 | async-start | bytes 1966080 | tf_op jit(solution)/shard_map/reduce_scatter | solution.py:162
  268.7 57.0 %copy-start.8 = (bf16[256,768]{1,0:T(8,128)(2,1)S(1)}, bf16[256,768]{1,0:T(8,128)(2,1)}, u32[]{:S(2)}) copy-start(bf16[256,768]{1,0:T(8,128)(2,1)} %reduce-scatter.18.cloned.1.call-done) | copy-start | bytes 1179652
  268.7 57.0 %copy-start.10 = (bf16[256,768]{1,0:T(8,128)(2,1)S(1)}, bf16[256,768]{1,0:T(8,128)(2,1)}, u32[]{:S(2)}) copy-start(bf16[256,768]{1,0:T(8,128)(2,1)} %reduce-scatter.22.cloned.1.call-done) | copy-start | bytes 1179652
  268.7 57.0 %copy-start.44 = (f32[768]{0:T(1024)S(1)}, f32[768]{0:T(1024)}, u32[]{:S(2)}) copy-start(f32[768]{0:T(1024)} %param.29) | copy-start | bytes 9220
  268.7 57.0 %copy-start.49 = (f32[256]{0:T(256)S(1)}, f32[256]{0:T(256)}, u32[]{:S(2)}) copy-start(f32[256]{0:T(256)} %copy-done.47) | copy-start | bytes 3076
  268.7 57.0 %copy-start.54 = (f32[256]{0:T(256)S(1)}, f32[256]{0:T(256)}, u32[]{:S(2)}) copy-start(f32[256]{0:T(256)} %get-tuple-element.358) | copy-start | bytes 3076
  268.7 57.0 %copy-start.56 = (f32[256]{0:T(256)S(1)}, f32[256]{0:T(256)}, u32[]{:S(2)}) copy-start(f32[256]{0:T(256)} %copy-done.55) | copy-start | bytes 3076
  268.7 57.0 %copy-start.57 = (f32[256]{0:T(256)S(1)}, f32[256]{0:T(256)}, u32[]{:S(2)}) copy-start(f32[256]{0:T(256)} %get-tuple-element.356) | copy-start | bytes 3076
  268.7 127.1 %reduce-scatter.30.cloned.1.call-start = ((), (), s32[]{:S(2)}) async-start(), calls=%async_computation.25 | async-start | bytes 1327104 | tf_op jit(solution)/shard_map/reduce_scatter | solution.py:282
  296.0 32.2 %copy-start.23 = (bf16[256,192]{1,0:T(8,128)(2,1)S(1)}, bf16[256,192]{1,0:T(8,128)(2,1)}, u32[]{:S(2)}) copy-start(bf16[256,192]{1,0:T(8,128)(2,1)} %copy-done.22) | copy-start | bytes 294916
  329.7 130.8 %reduce-scatter.40.cloned.1.call-start = ((), (), s32[]{:S(2)}) async-start(), calls=%async_computation.30 | async-start | bytes 884736
  360.8 20.0 %all-to-all-start.2 = ((bf16[2,8,64,192]{3,2,0,1:T(8,128)(2,1)}), bf16[2,8,64,192]{3,2,0,1:T(8,128)(2,1)S(1)}, u32[]{:S(2)}, u32[]{:S(2)}) async-start(bf16[2,8,64,192]{3,2,0,1:T(8,128)(2,1)} %copy.69), calls=%async_computation.6 | async-start | bytes 1048576 | tf_op jit(solution)/shard_map/all_to_all | solution.py:262
  366.3 122.5 %reduce-scatter.26.cloned.1.call-start = ((), (), s32[]{:S(2)}) async-start(), calls=%async_computation.23 | async-start | bytes 1310720 | tf_op jit(solution)/shard_map/reduce_scatter | solution.py:287
  387.4 127.2 %reduce-scatter.28.cloned.1.call-start = ((), (), s32[]{:S(2)}) async-start(), calls=%async_computation.24 | async-start | bytes 1310720 | tf_op jit(solution)/shard_map/reduce_scatter | solution.py:290
  392.7 143.4 %reduce-scatter.42.cloned.1.call-start = ((), (), s32[]{:S(2)}) async-start(), calls=%async_computation.31 | async-start | bytes 92160
  397.4 208.0 %reduce-scatter.34.cloned.1.call-start = ((), (), s32[]{:S(2)}) async-start(), calls=%async_computation.27 | async-start | bytes 1769472 | tf_op jit(solution)/shard_map/reduce_scatter | solution.py:279
  401.6 271.4 %reduce-scatter.36.cloned.1.call-start = ((), (), s32[]{:S(2)}) async-start(), calls=%async_computation.28 | async-start | bytes 1769472 | tf_op jit(solution)/shard_map/reduce_scatter | solution.py:280
  403.9 337.2 %reduce-scatter.38.cloned.1.call-start = ((), (), s32[]{:S(2)}) async-start(), calls=%async_computation.29 | async-start | bytes 1769472 | tf_op jit(solution)/shard_map/reduce_scatter | solution.py:281
  408.3 402.5 %reduce-scatter.32.cloned.1.call-start = ((), (), s32[]{:S(2)}) async-start(), calls=%async_computation.26 | async-start | bytes 2211840 | tf_op jit(solution)/shard_map/reduce_scatter | solution.py:277
  412.5 49.7 %copy-start.50 = (f32[768]{0:T(1024)S(1)}, f32[768]{0:T(1024)}, u32[]{:S(2)}) copy-start(f32[768]{0:T(1024)} %get-tuple-element.277) | copy-start | bytes 9220
  (58 other events, 516.1 us)
Sparse Core Ops, SparseCore 0:
  76.6 18.7 all-gather.3
  118.4 28.1 reduce-scatter.17
  150.5 19.6 all-gather.5
  181.3 28.1 reduce-scatter.21
  213.8 19.6 all-gather.7
  266.6 28.1 reduce-scatter.23
  297.4 28.1 reduce-scatter.19
  329.8 65.9 reduce-scatter.29
  399.1 61.3 reduce-scatter.39
  463.1 23.8 reduce-scatter.25
  489.6 25.0 reduce-scatter.27
  517.0 19.0 reduce-scatter.41
  540.5 64.8 reduce-scatter.33
  609.2 63.7 reduce-scatter.35
  677.2 63.7 reduce-scatter.37
  745.0 65.7 reduce-scatter.31
where the time goes:
time: 823 us; the launch traced here: 818 us
  waiting for transfers between devices  567 us (69%)
  local copies, waits for them, and re-layouts  78 us (9%)
  matrix products  64.8 us (8%)
  other arithmetic  45 us (5%)
  blocking collectives  25.2 us (3%)
  starting transfers between devices  18.2 us (2%)
  between operations  16.5 us (2%)
    reduce_scatter x1, waiting for transfers between devices, shards(): lax.psum_scatter(attend_grad, 'dp', scatter_dimension=0, tiled=True)  69.7 us
    reduce_scatter x1, waiting for transfers between devices, shards(): lax.psum_scatter(down_grad, 'dp', scatter_dimension=1, tiled=True)  68 us
    reduce_scatter x1, waiting for transfers between devices, shards(): lax.psum_scatter(gate_grad, 'dp', scatter_dimension=0, tiled=True)  67.9 us
    reduce_scatter x1, waiting for transfers between devices, shards(): lax.psum_scatter(up_grad, 'dp', scatter_dimension=0, tiled=True)  67.6 us
    unnamed x18, waiting for transfers between devices  65.6 us
    reduce_scatter x1, waiting for transfers between devices, shards(): lax.psum_scatter(jnp.dot(part_rows, down_weight, preferred_element_type=j...  29.6 us
    reduce_scatter x1, waiting for transfers between devices, shards(): lax.psum_scatter((jnp.dot(gate_back, gate_weight.T, preferred_element_typ...  28.3 us
    reduce_scatter x1, waiting for transfers between devices, shards(): lax.psum_scatter(jnp.dot(part_rows, output_weight, preferred_element_type...  28.3 us
  transfers between devices with their start and end apart: 19, of which 18 were waited for; matrix products, arithmetic and copies ran while one was open for 9% of the time, Pallas kernels for 0%

commit v1 on v0

--- a/solution.py
+++ b/solution.py
@@ -153,7 +153,24 @@
     ).astype(jnp.float32)
     after = inputs + branch_one
     normed_two, second_scale = normed_rows(after, second_gain)
-    normed_two_full = lax.all_gather(normed_two.astype(jnp.bfloat16), "tensor", axis=0, tiled=True)
+    x = normed_two.astype(jnp.bfloat16)
+    size, position_2, span = (lax.axis_size("tensor"), lax.axis_index("tensor"), x.shape[0])
+    route = [(i, (i + 1) % size) for i in range(size)]
+    behind = [(i, (i - 1) % size) for i in range(size)]
+    normed_two_full = jnp.zeros((*x.shape[:0], size * span, *x.shape[0 + 1 :]), x.dtype)
+    normed_two_full = lax.dynamic_update_slice_in_dim(normed_two_full, x, position_2 * span, axis=0)
+    from_left = from_right = x
+    half = size // 2
+    for step in range(1, half + 1):
+        from_left = lax.ppermute(from_left, "tensor", route)
+        normed_two_full = lax.dynamic_update_slice_in_dim(
+            normed_two_full, from_left, (position_2 - step) % size * span, axis=0
+        )
+        if step < size - half:
+            from_right = lax.ppermute(from_right, "tensor", behind)
+            normed_two_full = lax.dynamic_update_slice_in_dim(
+                normed_two_full, from_right, (position_2 + step) % size * span, axis=0
+            )
     gate = jnp.dot(normed_two_full, gate_weight, preferred_element_type=jnp.float32)
     up_part = jnp.dot(normed_two_full, up_weight, preferred_element_type=jnp.float32)
     sigmoid_gate = jax.nn.sigmoid(gate)

time: 823 us -> 823 us (level)
  waiting for transfers between devices: 567 us -> 554 us
    all_gather x1 -> x0, waiting for transfers between devices: 19.8 us -> none  [shards(): lax.all_gather(normed_two.astype(jnp.bfloat16), 'tensor', axis=0, tiled=T...]
    ppermute x0 -> x3, waiting for transfers between devices: none -> 11.7 us  [the longest x2 11.7 us: shards(): from_left = lax.ppermute(from_left, 'tensor', route)]
    unnamed x18 -> x17, waiting for transfers between devices: 65.6 us -> 64.4 us
  transfers between devices with their start and end apart: 19 -> 21, of which waited for: 18 -> 18; matrix products, arithmetic and copies ran while one was open for 9% -> 10% of each run, Pallas kernels for 0% -> 0%
where the time goes in v1:
time: 823 us; the launch traced here: 817 us
  waiting for transfers between devices  554 us (67%)
  local copies, waits for them, and re-layouts  81.6 us (10%)
  matrix products  68.2 us (8%)
  other arithmetic  48.8 us (6%)
  blocking collectives  25.3 us (3%)
  starting transfers between devices  19.9 us (2%)
  between operations  16.5 us (2%)
    reduce_scatter x1, waiting for transfers between devices, shards(): lax.psum_scatter(attend_grad, 'dp', scatter_dimension=0, tiled=True)  69.6 us
    reduce_scatter x1, waiting for transfers between devices, shards(): lax.psum_scatter(down_grad, 'dp', scatter_dimension=1, tiled=True)  68 us
    reduce_scatter x1, waiting for transfers between devices, shards(): lax.psum_scatter(up_grad, 'dp', scatter_dimension=0, tiled=True)  67.8 us
    reduce_scatter x1, waiting for transfers between devices, shards(): lax.psum_scatter(gate_grad, 'dp', scatter_dimension=0, tiled=True)  67.8 us
    unnamed x17, waiting for transfers between devices  64.4 us
    reduce_scatter x1, waiting for transfers between devices, shards(): lax.psum_scatter(jnp.dot(part_rows, down_weight, preferred_element_type=j...  29.5 us
    reduce_scatter x1, waiting for transfers between devices, shards(): lax.psum_scatter(jnp.dot(part_rows, output_weight, preferred_element_type...  28.3 us
    reduce_scatter x1, waiting for transfers between devices, shards(): lax.psum_scatter((jnp.dot(gate_back, gate_weight.T, preferred_element_typ...  27.9 us
  transfers between devices with their start and end apart: 21, of which 18 were waited for; matrix products, arithmetic and copies ran while one was open for 10% of the time, Pallas kernels for 0%

profile of v1, /device:TPU:0, one launch (start us, length us, event | category | flops | bytes accessed | tf_op | source)
XLA Modules:
  0.0 817.3 jit_solution(16036438366193117796)
XLA Ops:
  9.2 12.4 %scatter_fusion = s32[2,512]{1,0:T(2,128)S(1)} fusion(s32[2,512]{1,0:T(2,128)S(1)} %broadcast_in_dim.53, s32[256]{0:T(256)S(1)} %bitcast.157, s32[256]{0:T(256)S(1)} %get-tuple-element.364), kind=kCustom, calls=%fused_computation.4 | custom fusion | bytes 5120 | tf_op jit(solution)/shard_map/scatter | solution.py:97
  21.6 12.4 %scatter_fusion.1 = s32[2,512]{1,0:T(2,128)S(1)} fusion(s32[2,512]{1,0:T(2,128)S(1)} %scatter_fusion, s32[256]{0:T(256)S(1)} %bitcast.159, s32[256]{0:T(256)S(1)} %get-tuple-element.362), kind=kCustom, calls=%fused_computation.5 | custom fusion | bytes 5120 | tf_op jit(solution)/shard_map/scatter | solution.py:98
  34.7 7.3 all-to-all-start
  44.0 4.4 all-to-all-done
  58.8 13.2 %all-to-all-done.1 = bf16[2,8,64,192]{3,2,0,1:T(8,128)(2,1)S(1)} async-done(((bf16[2,8,64,192]{3,2,0,1:T(8,128)(2,1)}), bf16[2,8,64,192]{3,2,0,1:T(8,128)(2,1)S(1)}, u32[]{:S(2)}, u32[]{:S(2)}) %all-to-all-start.1) | async-done | bytes 393248 | tf_op jit(solution)/shard_map/all_to_all | solution.py:103
  77.5 17.7 %all-gather.3.cloned.1.call-done = bf16[1024,768]{1,0:T(8,128)(2,1)} async-done(((bf16[256,768]{1,0:T(8,128)(2,1)}), bf16[1024,768]{1,0:T(8,128)(2,1)}) %all-gather.3.cloned.1.call-update) | async-done | bytes 1572880 | tf_op jit(solution)/shard_map/all_gather | solution.py:110
  98.5 15.5 %while.30 = (s32[]{:T(128)}, bf16[2,512,3,64]{1,3,2,0:T(8,128)(2,1)S(1)}, f32[2,3,512]{2,1,0:T(4,128)S(1)}, s32[2]{0:T(128)S(1)}, s32[]{:T(128)}, /*index=5*/bf1...) while((s32[]{:T(128)}, ...), condition=%wide.region_8.9_spmd.clone.clone, body=%wide.region_5.8_spmd.clone.clone.sunk | while | flops 422674432 | bytes 22216908 | solution.py:145
  118.1 28.3 %reduce-scatter.18.cloned.1.call-done = bf16[256,768]{1,0:T(8,128)(2,1)} async-done(((bf16[1024,768]{1,0:T(8,128)(2,1)}), bf16[256,768]{1,0:T(8,128)(2,1)}) %reduce-scatter.18.cloned.1.call-update) | async-done | bytes 393232 | tf_op jit(solution)/shard_map/reduce_scatter | solution.py:148
  152.3 9.3 %collective-permute-done = bf16[256,768]{1,0:T(8,128)(2,1)S(1)} collective-permute-done((bf16[256,768]{1,0:T(8,128)(2,1)}, bf16[256,768]{1,0:T(8,128)(2,1)S(1)}, u32[]{:S(2)}, u32[]{:S(2)}) %collective-permute-start) | collective-permute-done | bytes 393248 | tf_op jit(solution)/shard_map/ppermute | solution.py:165
  173.2 4.3 multiply_convert_fusion.1
  181.4 27.9 %reduce-scatter.22.cloned.1.call-done = bf16[256,768]{1,0:T(8,128)(2,1)} async-done(((bf16[1024,768]{1,0:T(8,128)(2,1)}), bf16[256,768]{1,0:T(8,128)(2,1)}) %reduce-scatter.22.cloned.1.call-update) | async-done | bytes 393232 | tf_op jit(solution)/shard_map/reduce_scatter | solution.py:197
  213.4 19.7 %all-gather.5.cloned.1.call-done = bf16[1024,768]{1,0:T(8,128)(2,1)} async-done(((bf16[256,768]{1,0:T(8,128)(2,1)}), bf16[1024,768]{1,0:T(8,128)(2,1)}) %all-gather.5.cloned.1.call-update) | async-done | bytes 1572880 | tf_op jit(solution)/shard_map/all_gather | solution.py:210
  235.9 23.7 %while.31 = (s32[]{:T(128)}, f32[1024,3,64]{0,2,1:T(8,128)S(1)}, f32[1024,3,64]{0,2,1:T(8,128)}, bf16[2,512,3,64]{1,3,2,0:T(8,128)(2,1)}, s32[2]{0:T(128)S(1)}, ...) while((s32[]{:T(128)}, f32[1024,3,64]{0,2,1:T(8,128)S(1)}, ...), condition=%wide.region_16.17_spmd.clone.clone, body=%wide.region_14.16_spmd.clone.clone.sunk | while | flops 1032355840 | bytes 67424672 | solution.py:249
  268.7 25.8 %reduce-scatter.24.cloned.1.call-done = bf16[256,768]{1,0:T(8,128)(2,1)} async-done(((bf16[1024,768]{1,0:T(8,128)(2,1)}), bf16[256,768]{1,0:T(8,128)(2,1)}) %reduce-scatter.24.cloned.1.call-update) | async-done | bytes 393232 | tf_op jit(solution)/shard_map/reduce_scatter | solution.py:262
  295.7 29.5 %reduce-scatter.20.cloned.1.call-done = bf16[256,768]{1,0:T(8,128)(2,1)} async-done(((bf16[1024,768]{1,0:T(8,128)(2,1)}), bf16[256,768]{1,0:T(8,128)(2,1)}) %reduce-scatter.20.cloned.1.call-update) | async-done | bytes 393232 | tf_op jit(solution)/shard_map/reduce_scatter | solution.py:179
  333.2 13.1 %scatter_fusion.2 = f32[2,512,192]{2,1,0:T(8,128)S(1)} fusion(f32[2,512,192]{2,1,0:T(8,128)S(1)} %broadcast_in_dim.61, s32[256]{0:T(256)S(1)} %bitcast.158, f32[256,192]{1,0:T(8,128)S(1)} %get-tuple-element.349), kind=kCustom, calls=%fused_computation.6 | custom fusion | bytes 591872 | tf_op jit(solution)/shard_map/scatter | solution.py:276
  346.3 13.1 %scatter_fusion.3 = f32[2,512,192]{2,1,0:T(8,128)S(1)} fusion(f32[2,512,192]{2,1,0:T(8,128)S(1)} %scatter_fusion.2, s32[256]{0:T(256)S(1)} %bitcast.160, f32[256,192]{1,0:T(8,128)S(1)} %get-tuple-element.348), kind=kCustom, calls=%fused_computation.7 | custom fusion | bytes 591872 | tf_op jit(solution)/shard_map/scatter | solution.py:277
  360.4 5.5 all-to-all-start.2
  366.1 14.3 %all-to-all-done.2 = bf16[2,8,64,192]{3,2,0,1:T(8,128)(2,1)S(1)} async-done(((bf16[2,8,64,192]{3,2,0,1:T(8,128)(2,1)}), bf16[2,8,64,192]{3,2,0,1:T(8,128)(2,1)S(1)}, u32[]{:S(2)}, u32[]{:S(2)}) %all-to-all-start.2) | async-done | bytes 393248 | tf_op jit(solution)/shard_map/all_to_all | solution.py:279
  380.5 5.0 scatter_custom_fusion.4
  388.2 5.0 scatter_custom_fusion.5
  397.7 3.7 fusion.89
  409.3 4.1 fusion.88
  415.9 44.3 %reduce-scatter.40.cloned.1.call-done = f32[96,192]{1,0:T(8,128)} async-done(((f32[768,192]{1,0:T(8,128)}), f32[96,192]{1,0:T(8,128)}) %reduce-scatter.40.cloned.1.call-update) | async-done | bytes 73744
  461.9 19.6 %all-reduce.7 = (bf16[768]{0:T(1024)(128)(2,1)S(1)}, bf16[768]{0:T(1024)(128)(2,1)S(1)}) all-reduce(f32[768]{0:T(1024)S(1)} %get-tuple-element.279, f32[768]{0:T(1024)S(1)} %copy-done.51), channel_id=10, replica_groups=mesh['dp'=8,'tensor'=4] {'dp'}, use_global_device_ids=true, to_apply=%region_28.29.clone | all-reduce | flops 1536 | bytes 9216
  481.6 5.7 all-reduce.8
  490.4 23.9 %reduce-scatter.28.cloned.1.call-done = bf16[512,192]{1,0:T(8,128)(2,1)} async-done(((bf16[2048,192]{1,0:T(8,128)(2,1)}), bf16[512,192]{1,0:T(8,128)(2,1)}) %reduce-scatter.28.cloned.1.call-update) | async-done | bytes 196624 | tf_op jit(solution)/shard_map/reduce_scatter | solution.py:307
  516.1 19.8 %reduce-scatter.42.cloned.1.call-done = bf16[384,24]{0,1:T(8,128)(2,1)} async-done(((bf16[384,96]{0,1:T(8,128)(2,1)}), bf16[384,24]{0,1:T(8,128)(2,1)}) %reduce-scatter.42.cloned.1.call-update) | async-done | bytes 18448
  537.3 67.8 %reduce-scatter.34.cloned.1.call-done = f32[96,512]{1,0:T(8,128)} async-done(((f32[768,512]{1,0:T(8,128)}), f32[96,512]{1,0:T(8,128)}) %reduce-scatter.34.cloned.1.call-update) | async-done | bytes 196624 | tf_op jit(solution)/shard_map/reduce_scatter | solution.py:296
  605.0 67.8 %reduce-scatter.36.cloned.1.call-done = f32[96,512]{1,0:T(8,128)} async-done(((f32[768,512]{1,0:T(8,128)}), f32[96,512]{1,0:T(8,128)}) %reduce-scatter.36.cloned.1.call-update) | async-done | bytes 196624 | tf_op jit(solution)/shard_map/reduce_scatter | solution.py:297
  672.9 68.0 %reduce-scatter.38.cloned.1.call-done = f32[512,96]{0,1:T(8,128)} async-done(((f32[512,768]{0,1:T(8,128)}), f32[512,96]{0,1:T(8,128)}) %reduce-scatter.38.cloned.1.call-update) | async-done | bytes 196624 | tf_op jit(solution)/shard_map/reduce_scatter | solution.py:298
  740.9 69.6 %reduce-scatter.32.cloned.1.call-done = f32[96,576]{1,0:T(8,128)} async-done(((f32[768,576]{1,0:T(8,128)}), f32[96,576]{1,0:T(8,128)}) %reduce-scatter.32.cloned.1.call-update) | async-done | bytes 221200 | tf_op jit(solution)/shard_map/reduce_scatter | solution.py:294
  (329 shorter events, 135.2 us)
Async XLA Ops:
  7.2 88.1 %copy-start = (bf16[768,576]{0,1:T(8,128)(2,1)S(1)}, bf16[768,576]{0,1:T(8,128)(2,1)}, u32[]{:S(2)}) copy-start(bf16[768,576]{0,1:T(8,128)(2,1)} %param.27) | copy-start | bytes 2654212
  9.1 32.9 %copy-start.30 = (bf16[2048,192]{0,1:T(8,128)(2,1)S(1)}, bf16[2048,192]{0,1:T(8,128)(2,1)}, u32[]{:S(2)}) copy-start(bf16[2048,192]{0,1:T(8,128)(2,1)} %param.23) | copy-start | bytes 2359300
  34.7 13.7 %all-to-all-start = ((s32[8,1,128]{2,1,0:T(1,128)}), s32[8,1,128]{2,1,0:T(1,128)S(1)}, u32[]{:S(2)}, u32[]{:S(2)}) async-start(s32[8,1,128]{2,1,0:T(1,128)} %reshape.467), calls=%async_computation | async-start | bytes 8192 | tf_op jit(solution)/shard_map/all_to_all | solution.py:100
  55.1 16.9 %all-to-all-start.1 = ((bf16[2,8,64,192]{3,2,0,1:T(8,128)(2,1)}), bf16[2,8,64,192]{3,2,0,1:T(8,128)(2,1)S(1)}, u32[]{:S(2)}, u32[]{:S(2)}) async-start(bf16[2,8,64,192]{3,2,0,1:T(8,128)(2,1)} %pad_maximum_fusion.1), calls=%async_computation.1 | async-start | bytes 1048576 | tf_op jit(solution)/shard_map/all_to_all | solution.py:103
  58.7 36.6 %all-gather.3.cloned.1.call-start = ((), (), s32[]{:S(2)}) async-start(), calls=%async_computation.16 | async-start | bytes 1966080 | tf_op jit(solution)/shard_map/all_gather | solution.py:110
  76.3 70.0 %reduce-scatter.18.cloned.1.call-start = ((), (), s32[]{:S(2)}) async-start(), calls=%async_computation.17 | async-start | bytes 1966080 | tf_op jit(solution)/shard_map/reduce_scatter | solution.py:148
  118.0 91.2 %reduce-scatter.22.cloned.1.call-start = ((), (), s32[]{:S(2)}) async-start(), calls=%async_computation.19 | async-start | bytes 1966080 | tf_op jit(solution)/shard_map/reduce_scatter | solution.py:197
  150.5 11.1 %collective-permute-start = (bf16[256,768]{1,0:T(8,128)(2,1)}, bf16[256,768]{1,0:T(8,128)(2,1)S(1)}, u32[]{:S(2)}, u32[]{:S(2)}) collective-permute-start(bf16[256,768]{1,0:T(8,128)(2,1)} %get-tuple-element.324), channel_id=1, source_target_pairs={{0,1},{1,2},{2,3},{3,0},{4,5},{5,6},{6,7},{7,4},{8,9},{9,10},{10,1... | collective-permute-start | bytes 1179656 | tf_op jit(solution)/shard_map/ppermute | solution.py:165
  150.5 14.2 %collective-permute-start.1 = (bf16[256,768]{1,0:T(8,128)(2,1)}, bf16[256,768]{1,0:T(8,128)(2,1)}, u32[]{:S(2)}, u32[]{:S(2)}) collective-permute-start(bf16[256,768]{1,0:T(8,128)(2,1)} %get-tuple-element.324), channel_id=1, source_target_pairs={{0,3},{1,0},{2,1},{3,2},{4,7},{5,4},{6,5},{7,6},{8,11},{9,8},{10,9... | collective-permute-start | bytes 1179656 | tf_op jit(solution)/shard_map/ppermute | solution.py:170
  161.6 7.3 collective-permute-start.2
  181.1 52.0 %copy-start.40 = (bf16[192,768]{1,0:T(8,128)(2,1)S(1)}, bf16[192,768]{1,0:T(8,128)(2,1)}, u32[]{:S(2)}) copy-start(bf16[192,768]{1,0:T(8,128)(2,1)} %param.28) | copy-start | bytes 884740
  181.1 52.0 %all-gather.5.cloned.1.call-start = ((), (), s32[]{:S(2)}) async-start(), calls=%async_computation.20 | async-start | bytes 1966080 | tf_op jit(solution)/shard_map/all_gather | solution.py:210
  213.3 81.1 %reduce-scatter.24.cloned.1.call-start = ((), (), s32[]{:S(2)}) async-start(), calls=%async_computation.21 | async-start | bytes 1966080 | tf_op jit(solution)/shard_map/reduce_scatter | solution.py:262
  266.1 59.1 %reduce-scatter.20.cloned.1.call-start = ((), (), s32[]{:S(2)}) async-start(), calls=%async_computation.18 | async-start | bytes 1966080 | tf_op jit(solution)/shard_map/reduce_scatter | solution.py:179
  268.3 56.8 %copy-start.8 = (bf16[256,768]{1,0:T(8,128)(2,1)S(1)}, bf16[256,768]{1,0:T(8,128)(2,1)}, u32[]{:S(2)}) copy-start(bf16[256,768]{1,0:T(8,128)(2,1)} %reduce-scatter.18.cloned.1.call-done) | copy-start | bytes 1179652
  268.3 56.8 %copy-start.10 = (bf16[256,768]{1,0:T(8,128)(2,1)S(1)}, bf16[256,768]{1,0:T(8,128)(2,1)}, u32[]{:S(2)}) copy-start(bf16[256,768]{1,0:T(8,128)(2,1)} %reduce-scatter.22.cloned.1.call-done) | copy-start | bytes 1179652
  268.3 56.8 %copy-start.45 = (f32[768]{0:T(1024)S(1)}, f32[768]{0:T(1024)}, u32[]{:S(2)}) copy-start(f32[768]{0:T(1024)} %param.29) | copy-start | bytes 9220
  268.3 56.8 %copy-start.50 = (f32[256]{0:T(256)S(1)}, f32[256]{0:T(256)}, u32[]{:S(2)}) copy-start(f32[256]{0:T(256)} %copy-done.48) | copy-start | bytes 3076
  268.3 56.8 %copy-start.55 = (f32[256]{0:T(256)S(1)}, f32[256]{0:T(256)}, u32[]{:S(2)}) copy-start(f32[256]{0:T(256)} %get-tuple-element.360) | copy-start | bytes 3076
  268.4 56.8 %copy-start.57 = (f32[256]{0:T(256)S(1)}, f32[256]{0:T(256)}, u32[]{:S(2)}) copy-start(f32[256]{0:T(256)} %copy-done.56) | copy-start | bytes 3076
  268.4 56.8 %copy-start.58 = (f32[256]{0:T(256)S(1)}, f32[256]{0:T(256)}, u32[]{:S(2)}) copy-start(f32[256]{0:T(256)} %get-tuple-element.358) | copy-start | bytes 3076
  268.4 127.7 %reduce-scatter.30.cloned.1.call-start = ((), (), s32[]{:S(2)}) async-start(), calls=%async_computation.24 | async-start | bytes 1327104 | tf_op jit(solution)/shard_map/reduce_scatter | solution.py:299
  329.3 131.0 %reduce-scatter.40.cloned.1.call-start = ((), (), s32[]{:S(2)}) async-start(), calls=%async_computation.29 | async-start | bytes 884736
  360.4 20.0 %all-to-all-start.2 = ((bf16[2,8,64,192]{3,2,0,1:T(8,128)(2,1)}), bf16[2,8,64,192]{3,2,0,1:T(8,128)(2,1)S(1)}, u32[]{:S(2)}, u32[]{:S(2)}) async-start(bf16[2,8,64,192]{3,2,0,1:T(8,128)(2,1)} %copy.69), calls=%async_computation.6 | async-start | bytes 1048576 | tf_op jit(solution)/shard_map/all_to_all | solution.py:279
  365.9 122.7 %reduce-scatter.26.cloned.1.call-start = ((), (), s32[]{:S(2)}) async-start(), calls=%async_computation.22 | async-start | bytes 1310720 | tf_op jit(solution)/shard_map/reduce_scatter | solution.py:304
  388.2 126.1 %reduce-scatter.28.cloned.1.call-start = ((), (), s32[]{:S(2)}) async-start(), calls=%async_computation.23 | async-start | bytes 1310720 | tf_op jit(solution)/shard_map/reduce_scatter | solution.py:307
  396.0 139.9 %reduce-scatter.42.cloned.1.call-start = ((), (), s32[]{:S(2)}) async-start(), calls=%async_computation.30 | async-start | bytes 92160
  397.7 207.4 %reduce-scatter.34.cloned.1.call-start = ((), (), s32[]{:S(2)}) async-start(), calls=%async_computation.26 | async-start | bytes 1769472 | tf_op jit(solution)/shard_map/reduce_scatter | solution.py:296
  401.5 271.4 %reduce-scatter.36.cloned.1.call-start = ((), (), s32[]{:S(2)}) async-start(), calls=%async_computation.27 | async-start | bytes 1769472 | tf_op jit(solution)/shard_map/reduce_scatter | solution.py:297
  405.3 335.6 %reduce-scatter.38.cloned.1.call-start = ((), (), s32[]{:S(2)}) async-start(), calls=%async_computation.28 | async-start | bytes 1769472 | tf_op jit(solution)/shard_map/reduce_scatter | solution.py:298
  409.2 401.3 %reduce-scatter.32.cloned.1.call-start = ((), (), s32[]{:S(2)}) async-start(), calls=%async_computation.25 | async-start | bytes 2211840 | tf_op jit(solution)/shard_map/reduce_scatter | solution.py:294
  413.4 48.5 %copy-start.51 = (f32[768]{0:T(1024)S(1)}, f32[768]{0:T(1024)}, u32[]{:S(2)}) copy-start(f32[768]{0:T(1024)} %get-tuple-element.277) | copy-start | bytes 9220
  (61 other events, 567.4 us)
Sparse Core Ops, SparseCore 0:
  76.5 18.7 all-gather.2
  118.2 28.1 reduce-scatter.17
  181.2 27.9 reduce-scatter.21
  213.4 19.6 all-gather.4
  266.2 28.1 reduce-scatter.23
  297.0 28.1 reduce-scatter.19
  329.4 65.9 reduce-scatter.29
  398.7 61.4 reduce-scatter.39
  463.0 23.8 reduce-scatter.25
  489.2 25.0 reduce-scatter.27
  516.9 19.0 reduce-scatter.41
  540.2 64.8 reduce-scatter.33
  609.0 63.8 reduce-scatter.35
  677.1 63.7 reduce-scatter.37
  744.8 65.6 reduce-scatter.31
